TPU v7x, 32 devices: a whole 2x2x4 slice. The times are simulated.
32 devices in a mesh: rows: 8 (over y, x, core), loop: 4 (over z).
Axes of the slice: x: 2, y: 2, z: 4, core: 2. Of those that a mesh axis runs over, the one named last changes fastest.
Arguments:
- integrals: float32 [2, 2, 8192, 8192], P(None, None, 'rows', 'loop'), may hold values from -6 to 6
- mask: int32 [2, 64, 64], P(None, 'rows', 'loop'), may hold values 0 or 1
- coeffs: float32 [8192, 640], P('loop'), may hold values from -0.0625 to 0.0625
Outputs:
- exchange: float32 [8192, 8192], P('rows', 'loop')
All inputs are finite; a program needn't handle non-finite values. No bound on the sum of `mask` on one device may be relied on, other than what follows from the above.
Results may differ from a plain program's by a relative error of at most 0.00009.
Values sent between devices are 32-bit elements; how exact they have to be, the bound alone decides.
A program may use at most 192 MiB of HBM per device.

v0:
```python
import jax
import jax.numpy as jnp
from jax import lax
from jax.sharding import PartitionSpec as P

TILE = 128


def local(integrals, mask, coeffs):
    nslab, naux, mrows, lcols = integrals.shape
    blocks = mask.astype(jnp.float32)[:, None, :, None, :, None]
    shaped = integrals.reshape(nslab, naux, mrows // TILE, TILE, lcols // TILE, TILE)
    masked = (shaped * blocks).reshape(nslab * naux, mrows, lcols)
    norbit = coeffs.shape[1]
    loops = lax.axis_size("loop")
    row_count = lax.axis_size("rows")
    mine = norbit // loops
    ratio = row_count // loops
    depth = norbit * nslab * naux
    row_full = lax.psum(
        jnp.einsum("pml,li->ipm", masked, coeffs, precision=lax.Precision.HIGHEST), "loop"
    )
    own_orbits = lax.dynamic_slice_in_dim(row_full, lax.axis_index("loop") * mine, mine, 0)
    row_flat = row_full.reshape(depth, mrows)
    sub_rows = mrows // row_count
    split_rows = own_orbits.reshape(mine, nslab * naux, row_count, sub_rows)
    routed = lax.all_to_all(
        lax.all_to_all(split_rows, "rows", split_axis=2, concat_axis=2, tiled=True),
        "loop",
        split_axis=2,
        concat_axis=0,
        tiled=True,
    )
    piece = lax.all_gather(routed, "rows", axis=3, tiled=True)
    flat = piece.reshape(depth, ratio, piece.shape[3])
    tiles = jnp.einsum("dm,doc->moc", row_flat, flat, precision=lax.Precision.HIGHEST)
    total = tiles.reshape(mrows, lcols)
    scale = 1.0 / jnp.sqrt(jnp.float32(depth))
    return total * scale


def solution(mesh):
    in_specs = (P(None, None, "rows", "loop"), P(None, "rows", "loop"), P("loop", None))
    out_specs = P("rows", "loop")
    return jax.shard_map(local, mesh=mesh, in_specs=in_specs, out_specs=out_specs, check_vma=False)
```

profile of v0, /device:TPU:0, one launch (start us, length us, event | category | flops | bytes accessed | tf_op | source)
XLA Modules:
  0.0 881.7 jit_solution(2462211604459332383)
XLA Ops:
  6.5 0.0 all-reduce.2.cloned.1.call-start
  6.5 0.7 convert_element_type.3
  7.2 11.0 %mul.20 = f32[2,2,8,128,16,128]{5,4,3,2,1,0:T(8,128)} broadcast(f32[2,8,16]{2,1,0:T(8,128)S(1)} %convert_element_type.3), dimensions={0,2,4} | broadcast | bytes 33555456 | tf_op jit(solution)/shard_map/mul | solution.py:13
  18.3 35.5 %mul.21 = f32[4,1024,2048]{2,1,0:T(8,128)} reshape(f32[2,2,8,128,16,128]{5,4,3,2,1,0:T(8,128)} %mul.20) | data formatting | bytes 67108864 | tf_op jit(solution)/shard_map/mul | solution.py:13
  53.7 32.9 %bitcast_multiply_fusion = f32[4,1024,2048]{2,1,0:T(8,128)} fusion(f32[4,1024,2048]{2,1,0:T(8,128)} %mul.21, f32[2,2,1024,2048]{3,2,1,0:T(8,128)} %param.3), kind=kLoop, calls=%fused_computation | loop fusion | flops 8388608 | bytes 100663296 | tf_op jit(solution)/shard_map/mul | solution.py:13
  86.6 87.8 %fusion.2 = f32[640,4,1024]{0,2,1:T(8,128)} fusion(f32[4,1024,2048]{2,1,0:T(8,128)} %bitcast_multiply_fusion, f32[2048,640]{1,0:T(8,128)} %param.5), kind=kOutput, calls=%fused_computation.4 | convolution fusion | flops 64424509440 | bytes 49283072 | tf_op jit(solution)/shard_map/pml,li->ipm/dot_general | solution.py:21
  174.4 0.0 all-reduce.2.cloned.1.call-update
  174.5 0.2 all-gather.2.cloned.1.call-start
  174.7 361.1 %all-reduce.2.cloned.1.call-done = f32[640,4,1024]{0,2,1:T(8,128)} async-done(((f32[640,4,1024]{0,2,1:T(8,128)}), f32[640,4,1024]{0,2,1:T(8,128)}) %all-reduce.2.cloned.1.call-update) | async-done | bytes 10485776 | tf_op jit(solution)/shard_map/psum | solution.py:20
  535.8 5.9 constant_dynamic-slice_fusion
  541.7 4.1 copy.15
  545.9 35.6 %all_to_all.23 = f32[160,4,8,128]{3,0,1,2:T(8,128)S(1)} all-to-all(f32[160,4,8,128]{3,0,1,2:T(8,128)S(1)} %copy.15), channel_id=1, replica_groups=mesh['rows'=8,'loop'=4] {'rows'}, dimensions={2} | all-to-all | bytes 5242880 | tf_op jit(solution)/shard_map/all_to_all | solution.py:28
  581.5 61.6 %all_to_all.24 = f32[160,4,8,128]{3,0,1,2:T(8,128)S(1)} all-to-all(f32[160,4,8,128]{3,0,1,2:T(8,128)S(1)} %all_to_all.23), channel_id=1, replica_groups=mesh['rows'=8,'loop'=4] {'loop'}, dimensions={2} | all-to-all | bytes 5242880 | tf_op jit(solution)/shard_map/all_to_all | solution.py:27
  643.1 1.7 copy.17
  644.8 0.0 all-gather.2.cloned.1.call-update
  644.8 13.2 %copy.13 = f32[640,4,1024]{2,1,0:T(4,128)} copy(f32[640,4,1024]{0,2,1:T(8,128)} %all-reduce.2.cloned.1.call-done) | data formatting | bytes 20971520 | tf_op jit(solution)/shard_map/psum | solution.py:20
  658.1 12.4 %reshape.19 = f32[2560,1024]{1,0:T(8,128)} reshape(f32[640,4,1024]{2,1,0:T(4,128)} %copy.13) | data formatting | bytes 20971520 | tf_op jit(solution)/shard_map/reshape | solution.py:24
  670.4 84.0 %all-gather.2.cloned.1.call-done = f32[640,4,2,1024]{3,0,2,1:T(8,128)} async-done(((f32[640,4,2,128]{3,0,2,1:T(8,128)}), f32[640,4,2,1024]{3,0,2,1:T(8,128)}) %all-gather.2.cloned.1.call-update) | async-done | bytes 20971536 | tf_op jit(solution)/shard_map/all_gather | solution.py:34
  754.4 34.2 %copy.18 = f32[640,4,2,1024]{3,2,1,0:T(2,128)S(1)} copy(f32[640,4,2,1024]{3,0,2,1:T(8,128)} %all-gather.2.cloned.1.call-done) | data formatting | bytes 41943040 | tf_op jit(solution)/shard_map/all_gather | solution.py:34
  788.6 13.6 %copy.22 = f32[320,8,2,1024]{3,1,2,0:T(8,128)} copy(f32[320,8,2,1024]{3,2,1,0:T(2,128)S(1)} %bitcast.26) | data formatting | bytes 41943040
  802.2 72.6 %convolution_multiply_fusion = f32[1024,2048]{1,0:T(8,128)} fusion(f32[2560,1024]{1,0:T(8,128)} %reshape.19, f32[2048,2560]{0,1:T(8,128)} %bitcast.27), kind=kOutput, calls=%fused_computation.3 | convolution fusion | flops 64426606592 | bytes 39845888 | tf_op jit(solution)/shard_map/dm,doc->moc/dot_general | solution.py:36
Async XLA Ops:
  6.5 529.3 %all-reduce.2.cloned.1.call-start = ((), (), s32[]{:S(2)}) async-start(), calls=%async_computation.2 | async-start | bytes 20971520 | tf_op jit(solution)/shard_map/psum | solution.py:20
  174.5 580.0 %all-gather.2.cloned.1.call-start = ((), (), s32[]{:S(2)}) async-start(), calls=%async_computation.3 | async-start | bytes 23592960 | tf_op jit(solution)/shard_map/all_gather | solution.py:34
Sparse Core Ops, SparseCore 0:
  174.6 361.1 all-reduce.1
  645.0 109.4 all-gather.1
where the time goes:
time: 883 us; the launch traced here: 882 us
  waiting for transfers between devices  445 us (50%)
  matrix products  160 us (18%)
  local copies, waits for them, and re-layouts  132 us (15%)
  blocking collectives  97.3 us (11%)
  other arithmetic  33.6 us (4%)
  between operations  13.4 us (2%)
    psum x1, waiting for transfers between devices, local(): lax.psum(jnp.einsum('pml,li->ipm', masked, coeffs, precision=lax.Precisio...  361 us
    dot_general x1, matrix products, local(): jnp.einsum('pml,li->ipm', masked, coeffs, precision=lax.Precision.HIGHEST)  87.8 us
    all_gather x1, waiting for transfers between devices, local(): piece = lax.all_gather(routed, 'rows', axis=3, tiled=True)  84 us
    dot_general x1, matrix products, local(): jnp.einsum('dm,doc->moc', row_flat, flat, precision=lax.Precision.HIGHEST)  72.6 us
    all_to_all x1, blocking collectives, local(): lax.all_to_all(lax.all_to_all(split_rows, 'rows', split_axis=2, concat_ax...  61.6 us
    mul x2, local copies, waits for them, and re-layouts, local(): masked = (shaped * blocks).reshape(nslab * naux, mrows, lcols)  46.5 us
    all_to_all x1, blocking collectives, local(): lax.all_to_all(split_rows, 'rows', split_axis=2, concat_axis=2, tiled=True)  35.6 us
    all_gather x1, local copies, waits for them, and re-layouts, local(): piece = lax.all_gather(routed, 'rows', axis=3, tiled=True)  34.2 us
  transfers between devices with their start and end apart: 2, of which 2 were waited for; matrix products, arithmetic and copies ran while one was open for 3% of the time, Pallas kernels for 0%

commit v1 on v0

--- a/solution.py
+++ b/solution.py
@@ -17,8 +17,13 @@
     mine = norbit // loops
     ratio = row_count // loops
     depth = norbit * nslab * naux
-    row_full = lax.psum(
-        jnp.einsum("pml,li->ipm", masked, coeffs, precision=lax.Precision.HIGHEST), "loop"
+
+    def bring_the_racks(x0):
+        raw_out = jnp.sum(lax.all_gather(x0, "loop"), axis=0)
+        return raw_out
+
+    row_full = bring_the_racks(
+        jnp.einsum("pml,li->ipm", masked, coeffs, precision=lax.Precision.HIGHEST)
     )
     own_orbits = lax.dynamic_slice_in_dim(row_full, lax.axis_index("loop") * mine, mine, 0)
     row_flat = row_full.reshape(depth, mrows)

time: 883 us -> 1310 us (1.48)
  waiting for transfers between devices: 445 us -> 786 us
  local copies, waits for them, and re-layouts: 132 us -> 180 us
  other arithmetic: 33.6 us -> 65.4 us
    all_gather x0 -> x1, waiting for transfers between devices: none -> 702 us  [bring_the_racks(): raw_out = jnp.sum(lax.all_gather(x0, 'loop'), axis=0)]
    psum x1 -> x0, waiting for transfers between devices: 361 us -> none  [local(): lax.psum(jnp.einsum('pml,li->ipm', masked, coeffs, precision=lax.Precisio...]
    all_gather x0 -> x1, local copies, waits for them, and re-layouts: none -> 48.5 us  [bring_the_racks(): raw_out = jnp.sum(lax.all_gather(x0, 'loop'), axis=0)]
    reduce_sum x0 -> x1, other arithmetic: none -> 31.8 us  [bring_the_racks(): raw_out = jnp.sum(lax.all_gather(x0, 'loop'), axis=0)]
    reduce_sum x0 -> x1, local copies, waits for them, and re-layouts: none -> 13.2 us  [bring_the_racks(): raw_out = jnp.sum(lax.all_gather(x0, 'loop'), axis=0)]
    psum x1 -> x0, local copies, waits for them, and re-layouts: 13.2 us -> none  [local(): lax.psum(jnp.einsum('pml,li->ipm', masked, coeffs, precision=lax.Precisio...]
  transfers between devices with their start and end apart: 2 -> 2, of which waited for: 2 -> 2; matrix products, arithmetic and copies ran while one was open for 3% -> 2% of each run, Pallas kernels for 0% -> 0%
where the time goes in v1:
time: 1310 us; the launch traced here: 1300 us
  waiting for transfers between devices  786 us (60%)
  local copies, waits for them, and re-layouts  180 us (14%)
  matrix products  161 us (12%)
  blocking collectives  97.3 us (7%)
  other arithmetic  65.4 us (5%)
  between operations  13.8 us (1%)
    all_gather x1, waiting for transfers between devices, bring_the_racks(): raw_out = jnp.sum(lax.all_gather(x0, 'loop'), axis=0)  702 us
    dot_general x1, matrix products, local(): jnp.einsum('pml,li->ipm', masked, coeffs, precision=lax.Precision.HIGHEST)  87.8 us
    all_gather x1, waiting for transfers between devices, local(): piece = lax.all_gather(routed, 'rows', axis=3, tiled=True)  84 us
    dot_general x1, matrix products, local(): jnp.einsum('dm,doc->moc', row_flat, flat, precision=lax.Precision.HIGHEST)  72.8 us
    all_to_all x1, blocking collectives, local(): lax.all_to_all(lax.all_to_all(split_rows, 'rows', split_axis=2, concat_ax...  61.6 us
    all_gather x1, local copies, waits for them, and re-layouts, bring_the_racks(): raw_out = jnp.sum(lax.all_gather(x0, 'loop'), axis=0)  48.5 us
    mul x2, local copies, waits for them, and re-layouts, local(): masked = (shaped * blocks).reshape(nslab * naux, mrows, lcols)  46.5 us
    all_to_all x1, blocking collectives, local(): lax.all_to_all(split_rows, 'rows', split_axis=2, concat_axis=2, tiled=True)  35.6 us
  transfers between devices with their start and end apart: 2, of which 2 were waited for; matrix products, arithmetic and copies ran while one was open for 2% of the time, Pallas kernels for 0%

profile of v1, /device:TPU:0, one launch (start us, length us, event | category | flops | bytes accessed | tf_op | source)
XLA Modules:
  0.0 1303.8 jit_solution(8994078772651873090)
XLA Ops:
  6.5 0.0 all-gather.6.cloned.1.call-start
  6.5 0.7 convert_element_type.3
  7.2 11.0 mul.20
  18.3 35.5 %mul.21 = f32[4,1024,2048]{2,1,0:T(8,128)} reshape(f32[2,2,8,128,16,128]{5,4,3,2,1,0:T(8,128)} %mul.20) | data formatting | bytes 67108864 | tf_op jit(solution)/shard_map/mul | solution.py:13
  53.7 32.9 %bitcast_multiply_fusion = f32[4,1024,2048]{2,1,0:T(8,128)} fusion(f32[4,1024,2048]{2,1,0:T(8,128)} %mul.21, f32[2,2,1024,2048]{3,2,1,0:T(8,128)} %param.3), kind=kLoop, calls=%fused_computation | loop fusion | flops 8388608 | bytes 100663296 | tf_op jit(solution)/shard_map/mul | solution.py:13
  86.6 87.8 %fusion.2 = f32[640,4,1024]{0,2,1:T(8,128)} fusion(f32[4,1024,2048]{2,1,0:T(8,128)} %bitcast_multiply_fusion, f32[2048,640]{1,0:T(8,128)} %param.5), kind=kOutput, calls=%fused_computation.4 | convolution fusion | flops 64424509440 | bytes 49283072 | tf_op jit(solution)/shard_map/pml,li->ipm/dot_general | solution.py:26
  174.4 0.0 all-gather.6.cloned.1.call-update
  174.5 0.2 all-gather.4.cloned.1.call-start
  174.7 702.4 %all-gather.6.cloned.1.call-done = f32[2560,4,1024]{0,2,1:T(8,128)} async-done(((f32[640,4,1024]{0,2,1:T(8,128)}), f32[2560,4,1024]{0,2,1:T(8,128)}) %all-gather.6.cloned.1.call-update) | async-done | bytes 41943056 | tf_op jit(solution)/shard_map/all_gather | solution.py:22
  877.1 48.5 %reshape.22 = f32[4,640,4,1024]{1,0,3,2:T(4,128)} reshape(f32[2560,4,1024]{0,2,1:T(8,128)} %all-gather.6.cloned.1.call-done) | data formatting | bytes 83886080 | tf_op jit(solution)/shard_map/all_gather | solution.py:22
  925.5 31.8 %reduce_sum.9 = f32[640,4,1024]{0,2,1:T(8,128)} reduce(f32[4,640,4,1024]{1,0,3,2:T(4,128)} %reshape.22, f32[]{:T(128)} %constant.6.clone.1), dimensions={0}, to_apply=%region_0.0 | reduce | flops 7864320 | bytes 52428804 | tf_op jit(solution)/shard_map/reduce_sum | solution.py:22
  957.3 5.9 constant_dynamic-slice_fusion
  963.3 4.1 copy.15
  967.4 35.6 %all_to_all.23 = f32[160,4,8,128]{3,0,1,2:T(8,128)S(1)} all-to-all(f32[160,4,8,128]{3,0,1,2:T(8,128)S(1)} %copy.15), channel_id=1, replica_groups=mesh['rows'=8,'loop'=4] {'rows'}, dimensions={2} | all-to-all | bytes 5242880 | tf_op jit(solution)/shard_map/all_to_all | solution.py:33
  1003.0 61.6 %all_to_all.24 = f32[160,4,8,128]{3,0,1,2:T(8,128)S(1)} all-to-all(f32[160,4,8,128]{3,0,1,2:T(8,128)S(1)} %all_to_all.23), channel_id=1, replica_groups=mesh['rows'=8,'loop'=4] {'loop'}, dimensions={2} | all-to-all | bytes 5242880 | tf_op jit(solution)/shard_map/all_to_all | solution.py:32
  1064.7 1.7 copy.17
  1066.4 0.0 all-gather.4.cloned.1.call-update
  1066.4 13.2 %copy.13 = f32[640,4,1024]{2,1,0:T(4,128)} copy(f32[640,4,1024]{0,2,1:T(8,128)} %reduce_sum.9) | data formatting | bytes 20971520 | tf_op jit(solution)/shard_map/reduce_sum | solution.py:22
  1079.6 12.4 reshape.19
  1092.0 84.0 %all-gather.4.cloned.1.call-done = f32[640,4,2,1024]{3,0,2,1:T(8,128)} async-done(((f32[640,4,2,128]{3,0,2,1:T(8,128)}), f32[640,4,2,1024]{3,0,2,1:T(8,128)}) %all-gather.4.cloned.1.call-update) | async-done | bytes 20971536 | tf_op jit(solution)/shard_map/all_gather | solution.py:39
  1176.0 34.2 %copy.18 = f32[640,4,2,1024]{3,2,1,0:T(2,128)S(1)} copy(f32[640,4,2,1024]{3,0,2,1:T(8,128)} %all-gather.4.cloned.1.call-done) | data formatting | bytes 41943040 | tf_op jit(solution)/shard_map/all_gather | solution.py:39
  1210.2 13.6 %copy.22 = f32[320,8,2,1024]{3,1,2,0:T(8,128)} copy(f32[320,8,2,1024]{3,2,1,0:T(2,128)S(1)} %bitcast.28) | data formatting | bytes 41943040
  1223.8 72.8 %convolution_multiply_fusion = f32[1024,2048]{1,0:T(8,128)} fusion(f32[2560,1024]{1,0:T(8,128)} %reshape.19, f32[2048,2560]{0,1:T(8,128)} %bitcast.29), kind=kOutput, calls=%fused_computation.3 | convolution fusion | flops 64426606592 | bytes 39845888 | tf_op jit(solution)/shard_map/dm,doc->moc/dot_general | solution.py:41
Async XLA Ops:
  6.5 870.5 %all-gather.6.cloned.1.call-start = ((), (), s32[]{:S(2)}) async-start(), calls=%async_computation.3 | async-start | bytes 52428800 | tf_op jit(solution)/shard_map/all_gather | solution.py:22
  174.5 1001.5 %all-gather.4.cloned.1.call-start = ((), (), s32[]{:S(2)}) async-start(), calls=%async_computation.2 | async-start | bytes 23592960 | tf_op jit(solution)/shard_map/all_gather | solution.py:39
Sparse Core Ops, SparseCore 0:
  174.6 702.4 all-gather.5
  1066.5 109.4 all-gather.3
